TPU v7x, 256 devices: a whole 4x4x8 slice. The times are simulated.
256 devices in a mesh: dp: 8 (over x_lo, y), owner: 8 (over z), context: 4 (over x_hi, core).
Axes of the slice: x: 4 (x_hi: 2, x_lo: 2; x = x_hi * 2 + x_lo), y: 4, z: 8, core: 2. Of those that a mesh axis runs over, the one named last changes fastest.
Arguments:
- grad_partials: bfloat16 [32, 1536, 64, 192], P(('dp', 'context'), None, 'owner')
- assignment: int32 [64, 1], replicated, may hold values from 0 to 7; in each aligned block of 8 rows (0 to 7, 8 to 15, ...) at most 2 rows name the same one
- momentum: float32 [128, 1536, 192], P('owner', ('dp', 'context')), may hold values from -6 to 6
- q_weight: float32 [128, 1536, 192], P('owner', ('dp', 'context')), may hold values from -1.2 to 1.2
- k_weight: float32 [64, 512, 128], P('owner', ('dp', 'context')), may hold values from -6 to 6
- max_logits: float32 [4, 64], P('context'), may hold values from 20 to 400
Outputs:
- momentum_out: float32 [128, 1536, 192], P('owner', ('dp', 'context'))
- q_weight_out: float32 [128, 1536, 192], P('owner', ('dp', 'context'))
- k_weight_out: float32 [64, 512, 128], P('owner', ('dp', 'context'))
Inputs may be any that keep to these rules, and one draw needn't show every extreme that they name: `assignment`: in each aligned block of 8 heads no owner index is named more than 2 times, and some owner index exactly 2 times.
All inputs are finite; a program needn't handle non-finite values.
Results may differ from a plain program's by a relative error of at most 0.0007.
Values may be sent and summed in bfloat16 or wider, within the bound.
A program may use at most 128 MiB of HBM per device.

v0:
```python
import math
import jax
import jax.numpy as jnp
from jax import lax
from jax.sharding import PartitionSpec as P

QR = 1536
QK = 192
ITERS = 2
MOMENTUM_RATE = 0.95
WEIGHT_KEEP = 0.98
LOGIT_CAP = 100.0
QUINTIC_A = 3.4445
QUINTIC_B = -4.775
QUINTIC_C = 2.0315


def routing(assignment, heads_own, per_source):
    target = assignment[:, 0]
    head_index = jnp.arange(target.shape[0], dtype=jnp.int32)
    source_block = head_index // heads_own
    earlier = (
        (source_block[None, :] == source_block[:, None])
        & (head_index[None, :] < head_index[:, None])
        & (target[None, :] == target[:, None])
    )
    position = jnp.sum(earlier.astype(jnp.int32), axis=1)
    return (target, position, source_block * per_source + position)


def refresh(weight, orthogonal, gamma, kn_count):
    step_size = 0.04 * math.sqrt(max(QR, QK))
    column_index = jnp.arange(weight.shape[2])
    column_scale = jnp.where(
        column_index[None, :] < kn_count, jnp.sqrt(gamma)[:, None], gamma[:, None]
    )
    return (WEIGHT_KEEP * weight - step_size * orthogonal.astype(jnp.float32)) * column_scale[
        :, None, :
    ]


def quintic(whole):
    for step in range(ITERS):
        gram_matrix = jnp.einsum("nrk,nrl->nkl", whole, whole, preferred_element_type=jnp.float32)
        polynomial = (
            QUINTIC_B * gram_matrix
            + QUINTIC_C
            * jnp.einsum("nkl,nlm->nkm", gram_matrix, gram_matrix, precision=lax.Precision.HIGHEST)
        ).astype(jnp.bfloat16)
        whole = (
            QUINTIC_A * whole.astype(jnp.float32)
            + jnp.einsum("nrk,nkl->nrl", whole, polynomial, preferred_element_type=jnp.float32)
        ).astype(jnp.bfloat16)
    return whole


def orthogonalize(matrix):
    square_sum = lax.psum(jnp.sum(matrix * matrix, axis=(1, 2)), ("dp", "context"))
    iterate = (matrix / (jnp.sqrt(square_sum) + 1e-07)[:, None, None]).astype(jnp.bfloat16)
    row_count = matrix.shape[1]
    gathered = lax.all_gather(iterate, ("dp", "context"), axis=1, tiled=True)
    gathered = quintic(gathered)
    return lax.dynamic_slice_in_dim(
        gathered, lax.axis_index(("dp", "context")) * row_count, row_count, 1
    )


def body(grad_partials, assignment, momentum, q_weight, k_weight, max_logits):
    heads_own = grad_partials.shape[2]
    slots_own = momentum.shape[0]
    kn_count = k_weight.shape[2]
    per_source = slots_own // lax.axis_size("owner")
    my_owner = lax.axis_index("owner")
    target, position, local_slot = routing(assignment, heads_own, per_source)
    peak_logit = lax.pmax(max_logits[0], "context")
    gamma = jnp.minimum(1.0, LOGIT_CAP / peak_logit)
    partial_value = grad_partials[0]
    grad_rows = lax.psum_scatter(
        partial_value.astype(jnp.float32), ("dp", "context"), scatter_dimension=0, tiled=True
    )
    home_target = lax.dynamic_slice_in_dim(target, my_owner * heads_own, heads_own)
    home_position = lax.dynamic_slice_in_dim(position, my_owner * heads_own, heads_own)
    send_index = home_target * per_source + home_position
    slot_index = jnp.arange(slots_own, dtype=jnp.int32)
    sender = (slot_index[:, None] == send_index[None, :]).astype(jnp.float32)
    owned_mask = (
        (target[None, :] == my_owner) & (local_slot[None, :] == slot_index[:, None])
    ).astype(jnp.float32)
    occupied = (jnp.sum(owned_mask, axis=1) > 0.5)[:, None, None]
    home_gamma = lax.dynamic_slice_in_dim(gamma, my_owner * heads_own, heads_own)
    outgoing = jnp.einsum("qi,rik->qrk", sender, grad_rows, precision=lax.Precision.HIGHEST)
    arrived = lax.all_to_all(outgoing, "owner", split_axis=0, concat_axis=0, tiled=True)
    refreshed = jnp.where(occupied, MOMENTUM_RATE * momentum + arrived, momentum)
    orthogonal = orthogonalize(refreshed)
    slot_gamma = jnp.sum(owned_mask * gamma[None, :], axis=1)
    slot_gamma = jnp.where(occupied[:, 0, 0], slot_gamma, 1.0)
    q_weight_out = jnp.where(
        occupied, refresh(q_weight, orthogonal, slot_gamma, kn_count), q_weight
    )
    k_weight_out = k_weight * jnp.sqrt(home_gamma)[:, None, None]
    return (refreshed, q_weight_out, k_weight_out)


def solution(mesh):
    placed = (
        P(("dp", "context"), None, "owner", None),
        P(),
        P("owner", ("dp", "context"), None),
        P("owner", ("dp", "context"), None),
        P("owner", ("dp", "context"), None),
        P("context", None),
    )
    return jax.shard_map(
        body,
        mesh=mesh,
        in_specs=placed,
        out_specs=(
            P("owner", ("dp", "context"), None),
            P("owner", ("dp", "context"), None),
            P("owner", ("dp", "context"), None),
        ),
        check_vma=False,
    )
```

profile of v0, /device:TPU:1, one launch (start us, length us, event | category | flops | bytes accessed | tf_op | source)
XLA Modules:
  0.0 456.4 jit_solution(1013946448971146130)
XLA Ops:
  7.2 0.0 reduce-scatter.2.cloned.1.call-start
  7.2 9.2 %copy.57 = bf16[1,1536,8,192]{3,2,1,0:T(8,128)(2,1)} copy(bf16[1,1536,8,192]{1,3,2,0:T(8,128)(2,1)} %param.6) | data formatting | bytes 9437184 | tf_op args[0]
  16.4 7.5 %bitcast_convert_fusion = f32[1536,8,192]{2,1,0:T(8,128)} fusion(bf16[1,1536,8,192]{3,2,1,0:T(8,128)(2,1)} %copy.57), kind=kLoop, calls=%fused_computation.4 | loop fusion | flops 2359296 | bytes 14155776 | tf_op jit(solution)/shard_map/convert_element_type | solution.py:79
  23.8 0.0 copy-start.4
  23.8 0.0 reduce-scatter.2.cloned.1.call-update
  23.9 0.0 copy-start.5
  23.9 0.0 copy-start.1
  23.9 0.6 copy-done.4
  24.5 0.2 convert_reduce_fusion
  24.7 0.1 fusion.13
  24.7 175.2 %reduce-scatter.2.cloned.1.call-done = f32[48,8,192]{2,1,0:T(8,128)} async-done(((f32[1536,8,192]{2,1,0:T(8,128)}), f32[48,8,192]{2,1,0:T(8,128)}) %reduce-scatter.2.cloned.1.call-update) | async-done | bytes 294928 | tf_op jit(solution)/shard_map/reduce_scatter | solution.py:78
  199.9 1.6 fusion.8
  201.5 1.3 copy.58
  202.9 0.0 copy-start.3
  202.9 8.6 %all-to-all-start = ((f32[16,48,192]{2,1,0:T(8,128)}), f32[16,48,192]{2,1,0:T(8,128)S(1)}, u32[]{:S(2)}, u32[]{:S(2)}) async-start(f32[16,48,192]{2,1,0:T(8,128)} %copy.58), calls=%async_computation.1 | async-start | bytes 1572864 | tf_op jit(solution)/shard_map/all_to_all | solution.py:92
  211.5 0.0 all-gather.2.cloned.1.call-start
  211.5 0.0 copy-done.5
  211.5 10.9 %pmax.7 = f32[64]{0:T(128)S(1)} all-reduce(f32[64]{0:T(128)S(1)} %bitcast.24), channel_id=1, replica_groups=mesh['dp'=8,'owner'=8,'context'=4] {'context'}, use_global_device_ids=true, to_apply=%region_5.6 | all-reduce | flops 64 | bytes 512 | tf_op jit(solution)/shard_map/pmax | solution.py:75
  222.4 0.1 select_reduce_fusion
  222.5 8.9 %all-to-all-done = f32[16,48,192]{2,1,0:T(8,128)S(1)} async-done(((f32[16,48,192]{2,1,0:T(8,128)}), f32[16,48,192]{2,1,0:T(8,128)S(1)}, u32[]{:S(2)}, u32[]{:S(2)}) %all-to-all-start) | async-done | bytes 589856 | tf_op jit(solution)/shard_map/all_to_all | solution.py:92
  231.4 0.0 copy-done.1
  231.4 0.3 multiply_reduce_fusion
  231.7 0.0 copy-start
  231.8 66.2 %psum.7 = f32[16]{0:T(128)S(1)} all-reduce(f32[16]{0:T(128)S(1)} %get-tuple-element.16), channel_id=1, replica_groups=mesh['dp'=8,'owner'=8,'context'=4] {'dp','context'}, use_global_device_ids=true, to_apply=%region_4.5 | all-reduce | flops 16 | bytes 128 | tf_op jit(solution)/shard_map/psum | solution.py:58
  297.9 0.1 divide_convert_fusion
  298.1 0.9 copy.59
  298.9 0.0 all-gather.2.cloned.1.call-update
  299.0 0.1 dynamic-slice_sqrt_fusion
  299.1 0.1 broadcast_select_fusion
  299.1 0.0 copy-done.3
  299.1 0.7 broadcast_multiply_fusion
  299.9 73.1 %all-gather.2.cloned.1.call-done = bf16[16,1536,192]{2,0,1:T(8,128)(2,1)} async-done(((bf16[16,48,192]{2,0,1:T(8,128)(2,1)}), bf16[16,1536,192]{2,0,1:T(8,128)(2,1)}) %all-gather.2.cloned.1.call-update) | async-done | bytes 9437200 | tf_op jit(solution)/shard_map/all_gather | solution.py:61
  373.0 21.7 %fusion = f32[16,192,192]{2,1,0:T(8,128)S(1)} fusion(bf16[16,1536,192]{2,0,1:T(8,128)(2,1)} %all-gather.2.cloned.1.call-done), kind=kOutput, calls=%fused_computation.1 | convolution fusion | flops 1811939328 | bytes 11796480 | tf_op jit(solution)/shard_map/nrk,nrl->nkl/dot_general | solution.py:44
  394.7 0.0 copy-done
  394.7 3.6 add_convert_fusion.2
  398.3 17.7 %add_convert_fusion = bf16[16,1536,192]{2,1,0:T(8,128)(2,1)} fusion(bf16[16,192,192]{2,1,0:T(8,128)(2,1)S(1)} %add_convert_fusion.2, bf16[16,1536,192]{2,0,1:T(8,128)(2,1)} %all-gather.2.cloned.1.call-done), kind=kOutput, calls=%fused_computation | convolution fusion | flops 1830813696 | bytes 20054016 | tf_op jit(solution)/shard_map/nrk,nkl->nrl/dot_general | solution.py:52
  416.0 11.3 %fusion.15 = f32[16,192,192]{2,1,0:T(8,128)S(1)} fusion(bf16[16,1536,192]{2,1,0:T(8,128)(2,1)} %add_convert_fusion), kind=kOutput, calls=%fused_computation.44 | convolution fusion | flops 1811939328 | bytes 11796480 | tf_op jit(solution)/shard_map/nrk,nrl->nkl/dot_general | solution.py:44
  427.4 3.5 add_convert_fusion.1
  430.8 0.0 copy-start.2
  430.9 16.4 %fusion.16 = f32[16,1536,192]{2,1,0:T(8,128)} fusion(bf16[16,1536,192]{2,1,0:T(8,128)(2,1)} %add_convert_fusion, bf16[16,192,192]{2,1,0:T(8,128)(2,1)S(1)} %add_convert_fusion.1), kind=kOutput, calls=%fused_computation.45 | convolution fusion | flops 1811939328 | bytes 29491200 | tf_op jit(solution)/shard_map/nrk,nkl->nrl/dot_general | solution.py:52
  447.2 0.0 copy-done.2
  447.2 2.4 multiply_select_fusion
  (8 shorter events, 0.0 us)
Async XLA Ops:
  7.2 192.8 %reduce-scatter.2.cloned.1.call-start = ((), (), s32[]{:S(2)}) async-start(), calls=%async_computation.2 | async-start | bytes 12976128 | tf_op jit(solution)/shard_map/reduce_scatter | solution.py:78
  23.8 0.7 copy-start.4
  23.9 187.7 %copy-start.5 = (f32[1,64]{1,0:T(1,128)S(1)}, f32[1,64]{1,0:T(1,128)}, u32[]{:S(2)}) copy-start(f32[1,64]{1,0:T(1,128)} %param.11) | copy-start | bytes 772
  23.9 207.6 %copy-start.1 = (f32[16,48,192]{2,1,0:T(8,128)S(1)}, f32[16,48,192]{2,1,0:T(8,128)}, u32[]{:S(2)}) copy-start(f32[16,48,192]{2,1,0:T(8,128)} %param.8) | copy-start | bytes 1769476
  202.9 96.3 %copy-start.3 = (f32[8,16,128]{2,1,0:T(8,128)S(1)}, f32[8,16,128]{2,1,0:T(8,128)}, u32[]{:S(2)}) copy-start(f32[8,16,128]{2,1,0:T(8,128)} %param.10) | copy-start | bytes 196612
  202.9 28.6 %all-to-all-start = ((f32[16,48,192]{2,1,0:T(8,128)}), f32[16,48,192]{2,1,0:T(8,128)S(1)}, u32[]{:S(2)}, u32[]{:S(2)}) async-start(f32[16,48,192]{2,1,0:T(8,128)} %copy.58), calls=%async_computation.1 | async-start | bytes 1572864 | tf_op jit(solution)/shard_map/all_to_all | solution.py:92
  211.5 161.5 %all-gather.2.cloned.1.call-start = ((), (), s32[]{:S(2)}) async-start(), calls=%async_computation.3 | async-start | bytes 12976128 | tf_op jit(solution)/shard_map/all_gather | solution.py:61
  231.7 163.0 %copy-start = (f32[16,48,192]{2,1,0:T(8,128)}, f32[16,48,192]{2,1,0:T(8,128)S(1)}, u32[]{:S(2)}) copy-start(f32[16,48,192]{2,1,0:T(8,128)S(1)} %get-tuple-element.17) | copy-start | bytes 1769476
  430.8 16.4 %copy-start.2 = (f32[16,48,192]{2,1,0:T(8,128)S(1)}, f32[16,48,192]{2,1,0:T(8,128)}, u32[]{:S(2)}) copy-start(f32[16,48,192]{2,1,0:T(8,128)} %param.9) | copy-start | bytes 1769476
Sparse Core Ops, SparseCore 0:
  24.0 175.8 reduce-scatter.1
  299.1 73.8 all-gather.1
where the time goes:
time: 457 us; the launch traced here: 456 us
  waiting for transfers between devices  257 us (56%)
  blocking collectives  77 us (17%)
  matrix products  75.8 us (17%)
  between operations  14.2 us (3%)
  local copies, waits for them, and re-layouts  12.1 us (3%)
  other arithmetic  11.5 us (3%)
  starting transfers between devices  8.69 us (2%)
    reduce_scatter x1, waiting for transfers between devices, body(): lax.psum_scatter(partial_value.astype(jnp.float32), ('dp', 'context'), sc...  175 us
    all_gather x1, waiting for transfers between devices, orthogonalize(): gathered = lax.all_gather(iterate, ('dp', 'context'), axis=1, tiled=True)  73.1 us
    psum x1, blocking collectives, orthogonalize(): lax.psum(jnp.sum(matrix * matrix, axis=(1, 2)), ('dp', 'context'))  66.2 us
    dot_general x2, matrix products, quintic(): jnp.einsum('nrk,nkl->nrl', whole, polynomial, preferred_element_type=jnp....  34.1 us
    dot_general x2, matrix products, quintic(): jnp.einsum('nrk,nrl->nkl', whole, whole, preferred_element_type=jnp.float32)  33.1 us
    pmax x1, blocking collectives, body(): peak_logit = lax.pmax(max_logits[0], 'context')  10.9 us
    unnamed x13, local copies, waits for them, and re-layouts  9.79 us
  transfers between devices with their start and end apart: 3, of which 3 were waited for; matrix products, arithmetic and copies ran while one was open for 0% of the time, Pallas kernels for 0%

commit v1 on v0

--- a/solution.py
+++ b/solution.py
@@ -58,7 +58,12 @@
     square_sum = lax.psum(jnp.sum(matrix * matrix, axis=(1, 2)), ("dp", "context"))
     iterate = (matrix / (jnp.sqrt(square_sum) + 1e-07)[:, None, None]).astype(jnp.bfloat16)
     row_count = matrix.shape[1]
-    gathered = lax.all_gather(iterate, ("dp", "context"), axis=1, tiled=True)
+    gathered = jnp.concatenate(
+        lax.all_to_all(
+            jnp.stack([iterate] * lax.axis_size(("dp", "context"))), ("dp", "context"), 0, 0
+        ),
+        axis=1,
+    )
     gathered = quintic(gathered)
     return lax.dynamic_slice_in_dim(
         gathered, lax.axis_index(("dp", "context")) * row_count, row_count, 1

time: 457 us -> 565 us (1.24); the launches traced: 456 us -> 559 us
  waiting for transfers between devices: 257 us -> 355 us
  matrix products: 75.8 us -> 60 us
  local copies, waits for them, and re-layouts: 12.1 us -> 23.5 us
  starting transfers between devices: 8.69 us -> 17.4 us
    all_to_all x0 -> x1, waiting for transfers between devices: none -> 171 us  [orthogonalize(): lax.all_to_all(jnp.stack([iterate] * lax.axis_size(('dp', 'context'))), (...]
    all_gather x1 -> x0, waiting for transfers between devices: 73.1 us -> none  [orthogonalize(): gathered = lax.all_gather(iterate, ('dp', 'context'), axis=1, tiled=True)]
    dot_general x2, matrix products: 33.1 us -> 16.8 us  [quintic(): jnp.einsum('nrk,nrl->nkl', whole, whole, preferred_element_type=jnp.float32)]
    all_to_all x0 -> x1, starting transfers between devices: none -> 8.89 us  [orthogonalize(): lax.all_to_all(jnp.stack([iterate] * lax.axis_size(('dp', 'context'))), (...]
    reshape x0 -> x1, local copies, waits for them, and re-layouts: none -> 6.43 us  [orthogonalize(): jnp.concatenate(lax.all_to_all(jnp.stack([iterate] * lax.axis_size(('dp',...]
    another operation x0 -> x1, local copies, waits for them, and re-layouts: none -> 5.89 us  [orthogonalize(): jnp.stack([iterate] * lax.axis_size(('dp', 'context')))]
where the time goes in v1:
time: 565 us; the launch traced here: 559 us
  waiting for transfers between devices  355 us (63%)
  blocking collectives  77 us (14%)
  matrix products  60 us (11%)
  local copies, waits for them, and re-layouts  23.5 us (4%)
  starting transfers between devices  17.4 us (3%)
  between operations  14.2 us (3%)
  other arithmetic  11.5 us (2%)
    reduce_scatter x1, waiting for transfers between devices, body(): lax.psum_scatter(partial_value.astype(jnp.float32), ('dp', 'context'), sc...  175 us
    all_to_all x1, waiting for transfers between devices, orthogonalize(): lax.all_to_all(jnp.stack([iterate] * lax.axis_size(('dp', 'context'))), (...  171 us
    psum x1, blocking collectives, orthogonalize(): lax.psum(jnp.sum(matrix * matrix, axis=(1, 2)), ('dp', 'context'))  66.2 us
    dot_general x2, matrix products, quintic(): jnp.einsum('nrk,nkl->nrl', whole, polynomial, preferred_element_type=jnp....  30.6 us
    dot_general x2, matrix products, quintic(): jnp.einsum('nrk,nrl->nkl', whole, whole, preferred_element_type=jnp.float32)  16.8 us
  transfers between devices with their start and end apart: 3, of which 3 were waited for; matrix products, arithmetic and copies ran while one was open for 0% of the time, Pallas kernels for 0%

profile of v1, /device:TPU:1, one launch (start us, length us, event | category | flops | bytes accessed | tf_op | source)
XLA Modules:
  0.0 558.7 jit_solution(7918052659300187097)
XLA Ops:
  7.2 0.0 reduce-scatter.2.cloned.1.call-start
  7.2 9.2 %copy.86 = bf16[1,1536,8,192]{3,2,1,0:T(8,128)(2,1)} copy(bf16[1,1536,8,192]{1,3,2,0:T(8,128)(2,1)} %param.6) | data formatting | bytes 9437184 | tf_op args[0]
  16.4 7.5 %bitcast_convert_fusion = f32[1536,8,192]{2,1,0:T(8,128)} fusion(bf16[1,1536,8,192]{3,2,1,0:T(8,128)(2,1)} %copy.86), kind=kLoop, calls=%fused_computation.1 | loop fusion | flops 2359296 | bytes 14155776 | tf_op jit(solution)/shard_map/convert_element_type | solution.py:84
  23.8 0.0 copy-start.5
  23.8 0.0 reduce-scatter.2.cloned.1.call-update
  23.9 0.0 copy-start.6
  23.9 0.0 copy-start.2
  23.9 0.6 copy-done.5
  24.5 0.2 convert_reduce_fusion
  24.7 0.1 fusion.10
  24.7 175.2 %reduce-scatter.2.cloned.1.call-done = f32[48,8,192]{2,1,0:T(8,128)} async-done(((f32[1536,8,192]{2,1,0:T(8,128)}), f32[48,8,192]{2,1,0:T(8,128)}) %reduce-scatter.2.cloned.1.call-update) | async-done | bytes 294928 | tf_op jit(solution)/shard_map/reduce_scatter | solution.py:83
  199.9 1.6 fusion.5
  201.5 1.3 copy.87
  202.9 8.5 %all-to-all-start = ((f32[16,48,192]{2,1,0:T(8,128)}), f32[16,48,192]{2,1,0:T(8,128)S(1)}, u32[]{:S(2)}, u32[]{:S(2)}) async-start(f32[16,48,192]{2,1,0:T(8,128)} %copy.87), calls=%async_computation.1 | async-start | bytes 1572864 | tf_op jit(solution)/shard_map/all_to_all | solution.py:97
  211.3 0.0 copy-done.6
  211.3 10.9 %pmax.7 = f32[64]{0:T(128)S(1)} all-reduce(f32[64]{0:T(128)S(1)} %bitcast.31), channel_id=1, replica_groups=mesh['dp'=8,'owner'=8,'context'=4] {'context'}, use_global_device_ids=true, to_apply=%region_5.6 | all-reduce | flops 64 | bytes 512 | tf_op jit(solution)/shard_map/pmax | solution.py:80
  222.2 0.1 select_reduce_fusion
  222.4 8.9 %all-to-all-done = f32[16,48,192]{2,1,0:T(8,128)S(1)} async-done(((f32[16,48,192]{2,1,0:T(8,128)}), f32[16,48,192]{2,1,0:T(8,128)S(1)}, u32[]{:S(2)}, u32[]{:S(2)}) %all-to-all-start) | async-done | bytes 589856 | tf_op jit(solution)/shard_map/all_to_all | solution.py:97
  231.3 0.0 copy-done.2
  231.3 0.3 multiply_reduce_fusion
  231.6 0.0 copy-start.1
  231.6 66.2 %psum.7 = f32[16]{0:T(128)S(1)} all-reduce(f32[16]{0:T(128)S(1)} %get-tuple-element.22), channel_id=1, replica_groups=mesh['dp'=8,'owner'=8,'context'=4] {'dp','context'}, use_global_device_ids=true, to_apply=%region_4.5 | all-reduce | flops 16 | bytes 128 | tf_op jit(solution)/shard_map/psum | solution.py:58
  297.8 0.1 divide_convert_fusion
  297.9 5.9 %stack.2 = bf16[32,16,48,192]{3,2,1,0:T(8,128)(2,1)} broadcast(bf16[16,48,192]{2,1,0:T(8,128)(2,1)S(1)} %divide_convert_fusion), dimensions={1,2,3} | broadcast | bytes 9732096 | tf_op jit(solution)/shard_map/stack | solution.py:63
  303.8 0.0 copy-done.1
  303.8 0.0 copy-start.4
  303.8 8.9 %all-to-all-start.1 = ((bf16[32,16,48,192]{3,2,1,0:T(8,128)(2,1)}), bf16[32,16,48,192]{3,2,1,0:T(8,128)(2,1)}, u32[]{:S(2)}, u32[]{:S(2)}) async-start(bf16[32,16,48,192]{3,2,1,0:T(8,128)(2,1)} %stack.2), calls=%async_computation.2 | async-start | bytes 25165824 | tf_op jit(solution)/shard_map/all_to_all | solution.py:62
  312.7 0.1 dynamic-slice_sqrt_fusion
  312.8 0.1 broadcast_select_fusion
  312.9 0.0 copy-done.4
  312.9 0.7 broadcast_multiply_fusion
  313.6 171.0 %all-to-all-done.1 = bf16[32,16,48,192]{3,2,1,0:T(8,128)(2,1)} async-done(((bf16[32,16,48,192]{3,2,1,0:T(8,128)(2,1)}), bf16[32,16,48,192]{3,2,1,0:T(8,128)(2,1)}, u32[]{:S(2)}, u32[]{:S(2)}) %all-to-all-start.1) | async-done | bytes 9437216 | tf_op jit(solution)/shard_map/all_to_all | solution.py:62
  484.6 6.4 %copy.88 = bf16[16,32,48,192]{3,2,1,0:T(8,128)(2,1)S(1)} copy(bf16[16,32,48,192]{3,2,0,1:T(8,128)(2,1)} %bitcast.4) | data formatting | bytes 18874368 | tf_op jit(solution)/shard_map/reshape | solution.py:61
  491.1 0.0 copy-start
  491.1 5.5 fusion.12
  496.6 0.0 copy-done
  496.6 7.5 %add_convert_fusion.2 = bf16[16,192,192]{2,1,0:T(8,128)(2,1)S(1)} fusion(f32[16,192,192]{2,1,0:T(8,128)} %fusion.12), kind=kOutput, calls=%fused_computation.3 | convolution fusion | flops 1361313792 | bytes 3538944 | tf_op jit(solution)/shard_map/nkl,nlm->nkm/dot_general | solution.py:48
  504.1 14.2 %add_convert_fusion = bf16[16,1536,192]{2,1,0:T(8,128)(2,1)} fusion(bf16[16,1536,192]{2,1,0:T(8,128)(2,1)} %bitcast.29, bf16[16,192,192]{2,1,0:T(8,128)(2,1)S(1)} %add_convert_fusion.2), kind=kOutput, calls=%fused_computation | convolution fusion | flops 1830813696 | bytes 20054016 | tf_op jit(solution)/shard_map/nrk,nkl->nrl/dot_general | solution.py:52
  518.3 11.3 %fusion.13 = f32[16,192,192]{2,1,0:T(8,128)S(1)} fusion(bf16[16,1536,192]{2,1,0:T(8,128)(2,1)} %add_convert_fusion), kind=kOutput, calls=%fused_computation.42 | convolution fusion | flops 1811939328 | bytes 11796480 | tf_op jit(solution)/shard_map/nrk,nrl->nkl/dot_general | solution.py:44
  529.7 3.5 add_convert_fusion.1
  533.1 0.0 copy-start.3
  533.1 16.4 %fusion.14 = f32[16,1536,192]{2,1,0:T(8,128)} fusion(bf16[16,1536,192]{2,1,0:T(8,128)(2,1)} %add_convert_fusion, bf16[16,192,192]{2,1,0:T(8,128)(2,1)S(1)} %add_convert_fusion.1), kind=kOutput, calls=%fused_computation.43 | convolution fusion | flops 1811939328 | bytes 29491200 | tf_op jit(solution)/shard_map/nrk,nkl->nrl/dot_general | solution.py:52
  549.5 0.0 copy-done.3
  549.5 2.4 multiply_select_fusion
  (8 shorter events, 0.0 us)
Async XLA Ops:
  7.2 192.8 %reduce-scatter.2.cloned.1.call-start = ((), (), s32[]{:S(2)}) async-start(), calls=%async_computation.3 | async-start | bytes 12976128 | tf_op jit(solution)/shard_map/reduce_scatter | solution.py:83
  23.8 0.7 copy-start.5
  23.9 187.5 %copy-start.6 = (f32[1,64]{1,0:T(1,128)S(1)}, f32[1,64]{1,0:T(1,128)}, u32[]{:S(2)}) copy-start(f32[1,64]{1,0:T(1,128)} %param.11) | copy-start | bytes 772
  23.9 207.4 %copy-start.2 = (f32[16,48,192]{2,1,0:T(8,128)S(1)}, f32[16,48,192]{2,1,0:T(8,128)}, u32[]{:S(2)}) copy-start(f32[16,48,192]{2,1,0:T(8,128)} %param.8) | copy-start | bytes 1769476
  202.9 28.4 %all-to-all-start = ((f32[16,48,192]{2,1,0:T(8,128)}), f32[16,48,192]{2,1,0:T(8,128)S(1)}, u32[]{:S(2)}, u32[]{:S(2)}) async-start(f32[16,48,192]{2,1,0:T(8,128)} %copy.87), calls=%async_computation.1 | async-start | bytes 1572864 | tf_op jit(solution)/shard_map/all_to_all | solution.py:97
  231.6 72.2 %copy-start.1 = (f32[16,48,192]{2,1,0:T(8,128)}, f32[16,48,192]{2,1,0:T(8,128)S(1)}, u32[]{:S(2)}) copy-start(f32[16,48,192]{2,1,0:T(8,128)S(1)} %get-tuple-element.23) | copy-start | bytes 1769476
  303.8 9.1 %copy-start.4 = (f32[8,16,128]{2,1,0:T(8,128)S(1)}, f32[8,16,128]{2,1,0:T(8,128)}, u32[]{:S(2)}) copy-start(f32[8,16,128]{2,1,0:T(8,128)} %param.10) | copy-start | bytes 196612
  303.8 180.8 %all-to-all-start.1 = ((bf16[32,16,48,192]{3,2,1,0:T(8,128)(2,1)}), bf16[32,16,48,192]{3,2,1,0:T(8,128)(2,1)}, u32[]{:S(2)}, u32[]{:S(2)}) async-start(bf16[32,16,48,192]{3,2,1,0:T(8,128)(2,1)} %stack.2), calls=%async_computation.2 | async-start | bytes 25165824 | tf_op jit(solution)/shard_map/all_to_all | solution.py:62
  491.1 5.5 copy-start
  533.1 16.4 %copy-start.3 = (f32[16,48,192]{2,1,0:T(8,128)S(1)}, f32[16,48,192]{2,1,0:T(8,128)}, u32[]{:S(2)}) copy-start(f32[16,48,192]{2,1,0:T(8,128)} %param.9) | copy-start | bytes 1769476
Sparse Core Ops, SparseCore 0:
  24.0 175.8 reduce-scatter.1
